TPU v7x, 32 devices: a whole 2x2x4 slice. The times are simulated.
32 devices in a mesh: slides: 2 (over x), tok: 16 (over z, y, core).
Axes of the slice: x: 2, y: 2, z: 4, core: 2. Of those that a mesh axis runs over, the one named last changes fastest.
Arguments:
- queries: bfloat16 [8, 2048, 768], P('slides', 'tok'), parts along dimension 0, may hold values from -7 to 7
- key_rows: bfloat16 [8, 2048, 768], P('slides', 'tok'), parts along dimension 0, may hold values from -6 to 6
- value_rows: bfloat16 [8, 2048, 768], P('slides', 'tok'), parts along dimension 0, may hold values from -6 to 6
- projected_output_gradient: bfloat16 [8, 32768, 768], P('slides', 'tok'), parts along dimension 0, may hold values from -24 to 24
- out_weight: bfloat16 [768, 768], replicated, may hold values from -0.21875 to 0.21875
- offsets: int32 [16], replicated, may hold values from 0 to 15, each once
Outputs:
- grad_queries: bfloat16 [8, 2048, 768], P('slides', 'tok'), parts along dimension 0
- grad_keys: bfloat16 [8, 2048, 768], P('slides', 'tok'), parts along dimension 0
- grad_values: bfloat16 [8, 2048, 768], P('slides', 'tok'), parts along dimension 0
- grad_weight: float32 [1536, 768], P(('slides', 'tok')), parts along dimension 0
There are 2 independent parts, one for each index of `slides`. A program takes and returns all parts, laid end to end along the dimension named above; an argument that names none is the same for every part. Nothing has to cross between parts.
Inputs may be any that keep to these rules, and one draw needn't show every extreme that they name: offsets names each of the 16 phases once.
All inputs are finite; a program needn't handle non-finite values.
Results may differ from a plain program's by a relative error of at most 0.014.
Values may be sent and summed in bfloat16 or wider, within the bound.
A program may use at most 192 MiB of HBM per device.

v0:
```python
import functools

import jax
import jax.numpy as jnp
from jax import lax
from jax.experimental import pallas as pl
from jax.experimental.pallas import tpu as pltpu
from jax.sharding import PartitionSpec as P

MESH = pl.DeviceIdType.MESH
F32 = jnp.float32
BF16 = jnp.bfloat16
LOG2E = 1.4426950408889634


def dot(a, b, ca, cb):
    return lax.dot_general(a, b, (((ca,), (cb,)), ((), ())), preferred_element_type=F32)


def flip_bits(index, mask):
    out = index
    bit = 1
    while bit <= mask:
        if mask & bit:
            out = out + bit - 2 * bit * ((index // bit) % 2)
        bit *= 2
    return out


def main_kernel(
    dims,
    q_ref, k_ref, v_ref, w_ref, mask_ref, x_hbm,
    dq_ref, dk_ref, dv_ref, gw_ref,
    x, out_t, recv, res, ret, g_rows, spread, k_rows, v_rows, dk_acc, dv_acc, term, half, part, landed,
    x_sem, qkv_send, qkv_recv, g_send, g_recv, res_send, ret_recv, attn_send, attn_recv, red_send, red_recv,
):
    rounds, rows, width, heads, head_dim, tok, phases = dims
    seg = heads * rows
    me = lax.axis_index("tok")
    lane = me % heads
    base = me - lane
    order = sorted(range(1, heads), key=lambda s: (-(s // (heads // 2)), -s))
    scale = head_dim ** (-0.5)

    for r in range(rounds):
        pltpu.make_async_copy(x_hbm.at[r], x.at[r], x_sem.at[r]).start()

    greet = sorted(set(flip_bits_plain(heads)) | set(b for b in bits_of(tok)))
    barrier = pltpu.get_barrier_semaphore()
    for s in greet:
        peer = flip_bits(me, s)
        pl.semaphore_signal(barrier, inc=1, device_id={"tok": peer}, device_id_type=MESH)
    pl.semaphore_wait(barrier, len(greet))

    def columns(d):
        return pl.ds(pl.multiple_of(d * rows, rows), rows)

    def send_out(r, first, count, send_sem, recv_sem):
        for s in order:
            d = flip_bits(lane, s)
            pltpu.make_async_remote_copy(
                src_ref=out_t.at[r, pl.ds(first, count), d],
                dst_ref=recv.at[r, pl.ds(first, count), :, columns(lane)],
                send_sem=send_sem.at[r],
                recv_sem=recv_sem.at[r],
                device_id={"tok": base + d},
                device_id_type=MESH,
            ).start()
        pltpu.make_async_copy(
            out_t.at[r, pl.ds(first, count), lane],
            recv.at[r, pl.ds(first, count), :, columns(lane)],
            recv_sem.at[r],
        ).start()

    def prepare(r, carry):
        for a, ref in enumerate((q_ref, k_ref, v_ref)):
            out_t[r, a] = ref[r].T.reshape(heads, head_dim, rows)
        send_out(r, 0, 3, qkv_send, qkv_recv)
        pltpu.make_async_copy(x_hbm.at[r], x.at[r], x_sem.at[r]).wait()

        def chunk(c, inner):
            t = pl.multiple_of(c * 256, 256)
            y = dot(x[r, pl.ds(t, 256), :], w_ref[...], 1, 0)
            y = y.reshape(256 // phases, phases, width) * mask_ref[...][None]
            i = pl.multiple_of(c * (256 // phases), 256 // phases)
            g_rows[pl.ds(i, 256 // phases), :] = jnp.sum(y, axis=1).astype(BF16)
            return inner

        lax.fori_loop(0, rows * phases // 256, chunk, 0)
        out_t[r, 3] = g_rows[...].T.reshape(heads, head_dim, rows)
        send_out(r, 3, 1, g_send, g_recv)
        return carry

    lax.fori_loop(0, rounds, prepare, 0)

    def send_back(r, first, count, send_sem, recv_sem):
        for s in order:
            d = flip_bits(lane, s)
            pltpu.make_async_remote_copy(
                src_ref=res.at[r, pl.ds(first, count), :, columns(d)],
                dst_ref=ret.at[r, pl.ds(first, count), lane],
                send_sem=send_sem.at[r],
                recv_sem=recv_sem.at[r],
                device_id={"tok": base + d},
                device_id_type=MESH,
            ).start()
        pltpu.make_async_copy(
            res.at[r, pl.ds(first, count), :, columns(lane)],
            ret.at[r, pl.ds(first, count), lane],
            recv_sem.at[r],
        ).start()

    block = 256

    def attend(r, carry):
        pltpu.make_async_copy(
            recv.at[r, pl.ds(0, 3)], recv.at[r, pl.ds(0, 3)], qkv_recv.at[r]
        ).wait()
        k_rows[...] = recv[r, 1].T
        v_rows[...] = recv[r, 2].T
        dk_acc[...] = jnp.zeros_like(dk_acc)
        dv_acc[...] = jnp.zeros_like(dv_acc)
        pltpu.make_async_copy(recv.at[r, 3], recv.at[r, 3], g_recv.at[r]).wait()

        def q_block(b, inner):
            cols = pl.ds(pl.multiple_of(b * block, block), block)
            qt = recv[r, 0, :, cols]
            gt = recv[r, 3, :, cols]
            s = dot(k_rows[...], qt, 1, 0)
            top = jnp.max(s, axis=0, keepdims=True)
            e = jnp.exp2((s - top) * (scale * LOG2E))
            inv = 1.0 / jnp.sum(e, axis=0, keepdims=True)
            p = e * inv
            p_low = p.astype(BF16)
            ot = dot(recv[r, 2], p_low, 1, 0).astype(BF16)
            res[r, 3, :, cols] = ot
            dp = dot(v_rows[...], gt, 1, 0)
            delta = jnp.sum(gt.astype(F32) * ot.astype(F32), axis=0, keepdims=True)
            ds = (p * (dp - delta)).astype(BF16)
            res[r, 0, :, cols] = (dot(recv[r, 1], ds, 1, 0) * scale).astype(BF16)
            dk_acc[...] += dot(qt, ds, 1, 1)
            dv_acc[...] += dot(gt, p_low, 1, 1)
            return inner

        lax.fori_loop(0, seg // block, q_block, 0)
        res[r, 1] = (dk_acc[...] * scale).astype(BF16)
        res[r, 2] = dv_acc[...].astype(BF16)
        send_back(r, 3, 1, attn_send, attn_recv)
        send_back(r, 0, 3, res_send, ret_recv)
        return carry

    lax.fori_loop(0, rounds, attend, 0)

    term[...] = jnp.zeros_like(term)
    jb = 256

    def finish(r, carry):
        pltpu.make_async_copy(ret.at[r, 3], ret.at[r, 3], attn_recv.at[r]).wait()
        g_rows[...] = ret[r, 3].reshape(width, rows).T

        def chunk(c, inner):
            n = 256 // phases
            a = g_rows[pl.ds(pl.multiple_of(c * n, n), n), :].astype(F32)
            full = a[:, None, :] * mask_ref[...][None]
            spread[pl.ds(pl.multiple_of(c * 256, 256), 256), :] = full.reshape(256, width).astype(BF16)
            return inner

        lax.fori_loop(0, rows * phases // 256, chunk, 0)

        for j in range(width // jb):
            here = pl.ds(j * jb, jb)
            term[here, :] += dot(x[r, :, here], spread[...], 0, 0)
        return carry

    lax.fori_loop(0, rounds, finish, 0)

    def lay_out(r, carry):
        got = ret.at[r, pl.ds(0, 3)]
        pltpu.make_async_copy(got, got, ret_recv.at[r]).wait()
        for a, ref in enumerate((dq_ref, dk_ref, dv_ref)):
            ref[r] = ret[r, a].reshape(width, rows).T
        return carry

    lax.fori_loop(0, rounds - 1, lay_out, 0)

    own = width // tok
    part[...] = term[...].reshape(tok, own, width)
    count = tok
    stage = 0
    bit = 1
    at = 0
    kept = 0
    while bit < tok:
        b = (me // bit) % 2
        peer = me + bit - 2 * bit * b
        count //= 2
        for u in range(count):
            half[at + u] = part[kept + bit * (1 - b) + 2 * bit * u].astype(BF16)
        for u in range(count):
            pltpu.make_async_remote_copy(
                src_ref=half.at[at + u],
                dst_ref=landed.at[at + u],
                send_sem=red_send.at[at + u],
                recv_sem=red_recv.at[at + u],
                device_id={"tok": peer},
                device_id_type=MESH,
            ).start()
        kept = kept + bit * b
        if bit == 1:
            lay_out(rounds - 1, 0)
        for u in range(count):
            pltpu.make_async_remote_copy(
                src_ref=half.at[at + u],
                dst_ref=landed.at[at + u],
                send_sem=red_send.at[at + u],
                recv_sem=red_recv.at[at + u],
                device_id={"tok": peer},
                device_id_type=MESH,
            ).wait()
            part[kept + 2 * bit * u] += landed[at + u].astype(F32)
        at += count
        bit *= 2
    gw_ref[...] = part[me]

    for r in range(rounds):
        blocks = pl.ds(0, heads - 1)
        sent = out_t.at[r, pl.ds(0, 3), blocks]
        pltpu.make_async_copy(sent, sent, qkv_send.at[r]).wait()
        sent = out_t.at[r, pl.ds(3, 1), blocks]
        pltpu.make_async_copy(sent, sent, g_send.at[r]).wait()
        sent = ret.at[r, pl.ds(0, 3), blocks]
        pltpu.make_async_copy(sent, sent, res_send.at[r]).wait()
        sent = ret.at[r, pl.ds(3, 1), blocks]
        pltpu.make_async_copy(sent, sent, attn_send.at[r]).wait()


def flip_bits_plain(heads):
    return range(1, heads)


def bits_of(tok):
    bit = 1
    while bit < tok:
        yield bit
        bit *= 2


def local(queries, key_rows, value_rows, projected_output_gradient, out_weight, offsets):
    rounds, rows, width = queries.shape
    heads = offsets.shape[0]
    head_dim = width // heads
    tok = lax.axis_size("tok")
    phases = projected_output_gradient.shape[1] // rows
    seg = heads * rows
    own = width // tok
    dims = (rounds, rows, width, heads, head_dim, tok, phases)
    mask = (jnp.arange(phases)[:, None] == jnp.repeat(offsets, head_dim)[None, :]).astype(F32)
    vmem = pl.BlockSpec(memory_space=pltpu.VMEM)
    rows_shape = jax.ShapeDtypeStruct((rounds, rows, width), BF16)
    return pl.pallas_call(
        functools.partial(main_kernel, dims),
        out_shape=(rows_shape, rows_shape, rows_shape, jax.ShapeDtypeStruct((own, width), F32)),
        in_specs=[vmem] * 5 + [pl.BlockSpec(memory_space=pl.ANY)],
        out_specs=(vmem,) * 4,
        scratch_shapes=[
            pltpu.VMEM((rounds, rows * phases, width), BF16),
            pltpu.VMEM((rounds, 4, heads, head_dim, rows), BF16),
            pltpu.VMEM((rounds, 4, head_dim, seg), BF16),
            pltpu.VMEM((rounds, 4, head_dim, seg), BF16),
            pltpu.VMEM((rounds, 4, heads, head_dim, rows), BF16),
            pltpu.VMEM((rows, width), BF16),
            pltpu.VMEM((rows * phases, width), BF16),
            pltpu.VMEM((seg, head_dim), BF16),
            pltpu.VMEM((seg, head_dim), BF16),
            pltpu.VMEM((head_dim, seg), F32),
            pltpu.VMEM((head_dim, seg), F32),
            pltpu.VMEM((width, width), F32),
            pltpu.VMEM((tok, own, width), BF16),
            pltpu.VMEM((tok, own, width), F32),
            pltpu.VMEM((tok, own, width), BF16),
            pltpu.SemaphoreType.DMA((rounds,)),
            pltpu.SemaphoreType.DMA((rounds,)),
            pltpu.SemaphoreType.DMA((rounds,)),
            pltpu.SemaphoreType.DMA((rounds,)),
            pltpu.SemaphoreType.DMA((rounds,)),
            pltpu.SemaphoreType.DMA((rounds,)),
            pltpu.SemaphoreType.DMA((rounds,)),
            pltpu.SemaphoreType.DMA((rounds,)),
            pltpu.SemaphoreType.DMA((rounds,)),
            pltpu.SemaphoreType.DMA((tok,)),
            pltpu.SemaphoreType.DMA((tok,)),
        ],
        compiler_params=pltpu.CompilerParams(
            collective_id=0, has_side_effects=True, vmem_limit_bytes=64000000
        ),
        name="branch_backward",
    )(queries, key_rows, value_rows, out_weight, mask, projected_output_gradient)


def solution(mesh):
    placed = (
        P("slides", "tok", None),
        P("slides", "tok", None),
        P("slides", "tok", None),
        P("slides", "tok", None),
        P(),
        P(),
    )
    return jax.shard_map(
        local,
        mesh=mesh,
        in_specs=placed,
        out_specs=(
            P("slides", "tok", None),
            P("slides", "tok", None),
            P("slides", "tok", None),
            P(("slides", "tok"), None),
        ),
        check_vma=False,
    )
```

profile of v0, /device:TPU:0, one launch (start us, length us, event | category | flops | bytes accessed | tf_op | source)
XLA Modules:
  0.0 173.7 jit_solution(10807166356333272651)
XLA Ops:
  0.6 0.7 broadcast_in_dim.4
  1.4 0.1 eq.16
  1.4 0.6 fusion.mask_ref
  2.1 163.9 %branch_backward.1 = (bf16[4,128,768]{2,1,0:T(8,128)(2,1)}, bf16[4,128,768]{2,1,0:T(8,128)(2,1)}, bf16[4,128,768]{2,1,0:T(8,128)(2,1)}, f32[48,768]{1,0:T(8,128)}) custom-call(bf16[4,128,768]{2,1,0:T(8,128)(2,1)} %q_ref.1, bf16[4,128,768]{2,1,0:T(8,128)(2,1)} %k_ref.1, bf16[4,128,768]{2,1,0:T(8,128)(2,1)} %v_ref.1, bf16[768,768]{1,0:T(8,128)(2,1)} %w_ref.1, ...), custom_call_target="tpu_custom_call" | custom-call | tf_op jit(solution)/shard_map/branch_backward/pallas_call | solution.py:260
  165.9 2.1 %copy.14 = bf16[4,128,768]{2,1,0:T(8,128)(2,1)} copy(bf16[4,128,768]{2,1,0:T(8,128)(2,1)} %get-tuple-element.8) | data formatting | bytes 1572864
  168.0 2.1 %copy.15 = bf16[4,128,768]{2,1,0:T(8,128)(2,1)} copy(bf16[4,128,768]{2,1,0:T(8,128)(2,1)} %get-tuple-element.9) | data formatting | bytes 1572864
  170.1 2.1 %copy.16 = bf16[4,128,768]{2,1,0:T(8,128)(2,1)} copy(bf16[4,128,768]{2,1,0:T(8,128)(2,1)} %get-tuple-element.10) | data formatting | bytes 1572864
  172.1 1.6 copy.17
where the time goes:
time: 174 us
  Pallas kernels  164 us (94%)
  local copies, waits for them, and re-layouts  8.57 us (5%)
    pallas_call x1, Pallas kernels, local(): pl.pallas_call(functools.partial(main_kernel, dims), out_shape=(rows_shap...  164 us
    unnamed x4, local copies, waits for them, and re-layouts  7.77 us

commit v1 on v0

v1 whole, which is shorter than its diff:
```python
import functools

import jax
import jax.numpy as jnp
from jax import lax
from jax.experimental import pallas as pl
from jax.experimental.pallas import tpu as pltpu
from jax.sharding import PartitionSpec as P

MESH = pl.DeviceIdType.MESH
F32 = jnp.float32
BF16 = jnp.bfloat16
LOG2E = 1.4426950408889634
LANES = 128
PACK = 16


def dot(a, b, ca, cb):
    return lax.dot_general(a, b, (((ca,), (cb,)), ((), ())), preferred_element_type=F32)


def flip_bits(index, mask):
    out = index
    bit = 1
    while bit <= mask:
        if mask & bit:
            out = out + bit - 2 * bit * ((index // bit) % 2)
        bit *= 2
    return out


def main_kernel(
    dims,
    off_ref, q_hbm, k_hbm, v_hbm, w_hbm, x_hbm,
    dq_hbm, dk_hbm, dv_hbm, gw_hbm,
    x, qkv, w, wt, perm, out_t, recv, res, ret, kk, vv, vt1, acc, term, part, half, landed, cross_out, cross_in,
    laid, gw,
    x_sem, in_sem, w_sem, qkv_send, qkv_recv, g_send, g_recv, res_send, ret_recv, attn_send, attn_recv,
    red_send, red_recv, cross_send, cross_recv, out_sem, gw_sem,
):
    rounds, rows, width, heads, head_dim, tok, phases = dims
    seg = heads * rows
    me = lax.axis_index("tok")
    lane = me % heads
    base = me - lane
    order = sorted(range(1, heads), key=lambda s: (-(s // (heads // 2)), -s))
    scale = head_dim ** (-0.5)
    group = heads // 2
    groups = tok // group
    lo = me % group
    hi = me // group
    own = width // tok
    chunks = rows // PACK

    greet = sorted(set(range(1, heads)) | set(group * s for s in range(1, groups)))
    barrier = pltpu.get_barrier_semaphore()
    for s in greet:
        pl.semaphore_signal(barrier, inc=1, device_id={"tok": flip_bits(me, s)}, device_id_type=MESH)

    def load_qkv(r):
        return [
            pltpu.make_async_copy(ref.at[r], qkv.at[r, a], in_sem.at[r, a])
            for a, ref in enumerate((q_hbm, k_hbm, v_hbm))
        ]

    def load_x(r):
        return pltpu.make_async_copy(x_hbm.at[r], x.at[r], x_sem.at[r])

    load_w = pltpu.make_async_copy(w_hbm, w, w_sem)
    for r in range(rounds):
        for copy in load_qkv(r):
            copy.start()
        if r == 0:
            load_w.start()
        load_x(r).start()

    def columns(d):
        return pl.ds(pl.multiple_of(d * rows, rows), rows)

    def send_out(r, first, count, send_sem, recv_sem):
        for s in order:
            d = flip_bits(lane, s)
            pltpu.make_async_remote_copy(
                src_ref=out_t.at[r, pl.ds(first, count), d],
                dst_ref=recv.at[r, pl.ds(first, count), :, columns(lane)],
                send_sem=send_sem.at[r],
                recv_sem=recv_sem.at[r],
                device_id={"tok": base + d},
                device_id_type=MESH,
            ).start()
        pltpu.make_async_copy(
            out_t.at[r, pl.ds(first, count), lane],
            recv.at[r, pl.ds(first, count), :, columns(lane)],
            recv_sem.at[r],
        ).start()

    def turn(r):
        for a, copy in enumerate(load_qkv(r)):
            copy.wait()
            out_t[r, a] = qkv[r, a].T.reshape(heads, head_dim, rows)

    def project(r):
        load_x(r).wait()

        def chunk(c, inner):
            x[r, c] = dot(perm[...], x[r, c], 1, 0).astype(BF16)
            return inner

        lax.fori_loop(0, chunks, chunk, 0)
        for h in range(heads):
            chosen = x[r, :, h * PACK : (h + 1) * PACK, :].reshape(rows, width)
            out_t[r, 3, h] = dot(wt[h * head_dim : (h + 1) * head_dim, :], chosen, 1, 1).astype(BF16)

    turn(0)
    at = lax.broadcasted_iota(jnp.int32, (PACK, PACK * phases), 1)
    at = at - phases * lax.broadcasted_iota(jnp.int32, (PACK, PACK * phases), 0)
    for h in range(heads):
        perm[h * PACK : (h + 1) * PACK, :] = jnp.where(at == off_ref[h], 1.0, 0.0).astype(BF16)
    pl.semaphore_wait(barrier, len(greet))
    send_out(0, 0, 3, qkv_send, qkv_recv)
    load_w.wait()
    wt[...] = w[...].T

    def prepare(r, carry):
        project(r)
        send_out(r, 3, 1, g_send, g_recv)

        @pl.when(r + 1 < rounds)
        def _():
            turn(r + 1)
            send_out(r + 1, 0, 3, qkv_send, qkv_recv)

        return carry

    lax.fori_loop(0, rounds, prepare, 0)

    def send_back(r, a, send_sem, recv_sem):
        for s in order:
            d = flip_bits(lane, s)
            pltpu.make_async_remote_copy(
                src_ref=res.at[r, a, :, columns(d)],
                dst_ref=ret.at[r, a, lane],
                send_sem=send_sem,
                recv_sem=recv_sem,
                device_id={"tok": base + d},
                device_id_type=MESH,
            ).start()
        pltpu.make_async_copy(res.at[r, a, :, columns(lane)], ret.at[r, a, lane], recv_sem).start()

    def send_grads(r):
        for a in range(3):
            send_back(r, a, res_send.at[r, a], ret_recv.at[r, a])

    block = seg // 2
    k_pad = jnp.zeros((LANES - 2 * head_dim, seg), BF16)
    v_pad = jnp.zeros((LANES - head_dim - PACK, seg), BF16)
    ones = jnp.ones((PACK, seg), BF16)

    def attend(r, carry):
        got = recv.at[r, pl.ds(0, 3)]
        pltpu.make_async_copy(got, got, qkv_recv.at[r]).wait()
        kt = recv[r, 1]
        vt = recv[r, 2]
        kk[...] = jnp.concatenate([kt, kt, k_pad], 0).T
        vv[...] = jnp.concatenate([vt, ones, v_pad], 0).T
        vt1[...] = jnp.concatenate([vt, ones], 0)
        acc[...] = jnp.zeros_like(acc)
        pltpu.make_async_copy(recv.at[r, 3], recv.at[r, 3], g_recv.at[r]).wait()

        def q_block(b, inner):
            cols = pl.ds(pl.multiple_of(b * block, block), block)
            qt = recv[r, 0, :, cols].astype(F32)
            gt = recv[r, 3, :, cols]
            gf = gt.astype(F32)
            qc = qt * (scale * LOG2E)
            q_high = qc.astype(BF16)
            q_low = (qc - q_high.astype(F32)).astype(BF16)
            q_two = jnp.concatenate([q_high, q_low, jnp.zeros((LANES - 2 * head_dim, block), BF16)], 0)
            s = dot(kk[...], q_two, 1, 0)
            e = jnp.exp2(s - jnp.max(s, axis=0, keepdims=True)).astype(BF16)
            both = dot(vt1[...], e, 1, 0)
            inv = 1.0 / both[head_dim : head_dim + 1]
            ot = (both[:head_dim] * inv).astype(BF16)
            res[r, 3, :, cols] = ot
            minus = -jnp.sum(gf * ot.astype(F32), axis=0, keepdims=True)
            m_high = minus.astype(BF16).astype(F32)
            row = lax.broadcasted_iota(jnp.int32, (PACK, block), 0)
            m_two = jnp.where(row == 0, m_high, jnp.where(row == 1, minus - m_high, 0.0)).astype(BF16)
            g_two = jnp.concatenate([gt, m_two, jnp.zeros((LANES - head_dim - PACK, block), BF16)], 0)
            ds = e * dot(vv[...], g_two, 1, 0).astype(BF16)
            res[r, 0, :, cols] = (dot(kt, ds, 1, 0) * (inv * scale)).astype(BF16)
            qs = (qt * (inv * scale)).astype(BF16)
            gs = (gf * inv).astype(BF16)
            zero = jnp.zeros((head_dim, block), BF16)
            right = jnp.concatenate(
                [
                    jnp.concatenate([gs, zero], 1),
                    jnp.concatenate([zero, qs], 1),
                    jnp.zeros((LANES - 2 * head_dim, 2 * block), BF16),
                ],
                0,
            )
            acc[...] += dot(jnp.concatenate([e, ds], 1), right, 1, 1)
            return inner

        lax.fori_loop(0, seg // block, q_block, 0)
        send_back(r, 3, attn_send.at[r], attn_recv.at[r])
        t = acc[...].astype(BF16).T
        res[r, 2] = t[:head_dim]
        res[r, 1] = t[head_dim : 2 * head_dim]

        @pl.when(r == 1)
        def _():
            send_grads(0)

        return carry

    lax.fori_loop(0, rounds, attend, 0)
    send_grads(1)

    term[...] = jnp.zeros_like(term)

    def finish(r, carry):
        pltpu.make_async_copy(ret.at[r, 3], ret.at[r, 3], attn_recv.at[r]).wait()
        for h in range(heads):
            chosen = x[r, :, h * PACK : (h + 1) * PACK, :].reshape(rows, width)
            here = pl.ds(h * head_dim, head_dim)
            term[here, :] += dot(ret[r, 3, h], chosen, 1, 0)
        return carry

    lax.fori_loop(0, rounds, finish, 0)
    part[...] = term[...].T.reshape(groups, group, own, width)
    half[...] = part[...].astype(BF16)

    def near(s):
        return pltpu.make_async_remote_copy(
            src_ref=half.at[:, flip_bits(lo, s)],
            dst_ref=landed.at[lo],
            send_sem=red_send.at[s],
            recv_sem=red_recv.at[s],
            device_id={"tok": hi * group + flip_bits(lo, s)},
            device_id_type=MESH,
        )

    def far(s):
        return pltpu.make_async_remote_copy(
            src_ref=cross_out.at[flip_bits(hi, s)],
            dst_ref=cross_in.at[hi],
            send_sem=cross_send.at[s],
            recv_sem=cross_recv.at[s],
            device_id={"tok": flip_bits(hi, s) * group + lo},
            device_id_type=MESH,
        )

    def lay_out(r):
        for a, ref in enumerate((dq_hbm, dk_hbm, dv_hbm)):
            pltpu.make_async_copy(ret.at[r, a], ret.at[r, a], ret_recv.at[r, a]).wait()
            laid[r, a] = ret[r, a].reshape(width, rows).T
            pltpu.make_async_copy(laid.at[r, a], ref.at[r], out_sem.at[r, a]).start()

    for s in range(1, group):
        near(s).start()
    for r in range(2, rounds - 1):
        send_grads(r)
    lay_out(0)
    for s in range(1, group):
        near(s).wait()
    for j in range(groups):
        total = part[j, lo]
        for s in range(1, group):
            total = total + landed[flip_bits(lo, s), j].astype(F32)
        part[j, lo] = total
        cross_out[j] = total.astype(BF16)
    for s in range(1, groups):
        far(s).start()
    send_grads(rounds - 1)
    for r in range(1, rounds - 1):
        lay_out(r)
    for s in range(1, groups):
        far(s).wait()
    total = part[hi, lo]
    for s in range(1, groups):
        total = total + cross_in[flip_bits(hi, s)].astype(F32)
    gw[...] = total
    pltpu.make_async_copy(gw, gw_hbm, gw_sem).start()
    lay_out(rounds - 1)

    for r in range(rounds):
        blocks = pl.ds(0, heads - 1)
        sent = out_t.at[r, pl.ds(0, 3), blocks]
        pltpu.make_async_copy(sent, sent, qkv_send.at[r]).wait()
        sent = out_t.at[r, 3, blocks]
        pltpu.make_async_copy(sent, sent, g_send.at[r]).wait()
        for a in range(3):
            sent = ret.at[r, a, blocks]
            pltpu.make_async_copy(sent, sent, res_send.at[r, a]).wait()
        sent = ret.at[r, 3, blocks]
        pltpu.make_async_copy(sent, sent, attn_send.at[r]).wait()
    for r in range(rounds):
        for a, ref in enumerate((dq_hbm, dk_hbm, dv_hbm)):
            pltpu.make_async_copy(laid.at[r, a], ref.at[r], out_sem.at[r, a]).wait()
    pltpu.make_async_copy(gw, gw_hbm, gw_sem).wait()


def hand_over(*refs):
    count = (len(refs) - 2) // 3
    got, given, kept = refs[:count], refs[count : 2 * count], refs[2 * count : 3 * count]
    in_sem, out_sem = refs[3 * count :]
    into = [pltpu.make_async_copy(got[i], kept[i], in_sem.at[i]) for i in range(count)]
    out_of = [pltpu.make_async_copy(kept[i], given[i], out_sem.at[i]) for i in range(count)]
    for copy in into:
        copy.start()
    for i in range(count):
        into[i].wait()
        out_of[i].start()
    for copy in out_of:
        copy.wait()


def local(queries, key_rows, value_rows, projected_output_gradient, out_weight, offsets):
    rounds, rows, width = queries.shape
    heads = offsets.shape[0]
    head_dim = width // heads
    tok = lax.axis_size("tok")
    phases = projected_output_gradient.shape[1] // rows
    seg = heads * rows
    own = width // tok
    group = heads // 2
    groups = tok // group
    dims = (rounds, rows, width, heads, head_dim, tok, phases)
    tokens = projected_output_gradient.reshape(rounds, rows // PACK, PACK * phases, width)
    hbm = pl.BlockSpec(memory_space=pl.ANY)
    rows_shape = jax.ShapeDtypeStruct((rounds, rows, width), BF16)
    out_shape = (rows_shape, rows_shape, rows_shape, jax.ShapeDtypeStruct((own, width), F32))
    dma = pltpu.SemaphoreType.DMA
    results = pl.pallas_call(
        functools.partial(main_kernel, dims),
        out_shape=out_shape,
        in_specs=[pl.BlockSpec(memory_space=pltpu.SMEM)] + [hbm] * 5,
        out_specs=(hbm,) * 4,
        scratch_shapes=[
            pltpu.VMEM((rounds, rows // PACK, PACK * phases, width), BF16),
            pltpu.VMEM((rounds, 3, rows, width), BF16),
            pltpu.VMEM((width, width), BF16),
            pltpu.VMEM((width, width), BF16),
            pltpu.VMEM((PACK * heads, PACK * phases), BF16),
            pltpu.VMEM((rounds, 4, heads, head_dim, rows), BF16),
            pltpu.VMEM((rounds, 4, head_dim, seg), BF16),
            pltpu.VMEM((rounds, 4, head_dim, seg), BF16),
            pltpu.VMEM((rounds, 4, heads, head_dim, rows), BF16),
            pltpu.VMEM((seg, LANES), BF16),
            pltpu.VMEM((seg, LANES), BF16),
            pltpu.VMEM((head_dim + PACK, seg), BF16),
            pltpu.VMEM((seg, LANES), F32),
            pltpu.VMEM((width, width), F32),
            pltpu.VMEM((groups, group, own, width), F32),
            pltpu.VMEM((groups, group, own, width), BF16),
            pltpu.VMEM((group, groups, own, width), BF16),
            pltpu.VMEM((groups, own, width), BF16),
            pltpu.VMEM((groups, own, width), BF16),
            pltpu.VMEM((rounds, 3, rows, width), BF16),
            pltpu.VMEM((own, width), F32),
            dma((rounds,)),
            dma((rounds, 3)),
            dma,
            dma((rounds,)),
            dma((rounds,)),
            dma((rounds,)),
            dma((rounds,)),
            dma((rounds, 3)),
            dma((rounds, 3)),
            dma((rounds,)),
            dma((rounds,)),
            dma((group,)),
            dma((group,)),
            dma((groups,)),
            dma((groups,)),
            dma((rounds, 3)),
            dma,
        ],
        compiler_params=pltpu.CompilerParams(
            collective_id=0, has_side_effects=True, vmem_limit_bytes=66000000
        ),
        name="branch_backward",
    )(offsets, queries, key_rows, value_rows, out_weight, tokens)
    return pl.pallas_call(
        hand_over,
        out_shape=out_shape,
        in_specs=[hbm] * 4,
        out_specs=(hbm,) * 4,
        scratch_shapes=[pltpu.VMEM(a.shape, a.dtype) for a in out_shape] + [dma((4,)), dma((4,))],
        name="hand_over",
    )(*results)


def solution(mesh):
    placed = (
        P("slides", "tok", None),
        P("slides", "tok", None),
        P("slides", "tok", None),
        P("slides", "tok", None),
        P(),
        P(),
    )
    return jax.shard_map(
        local,
        mesh=mesh,
        in_specs=placed,
        out_specs=(
            P("slides", "tok", None),
            P("slides", "tok", None),
            P("slides", "tok", None),
            P(("slides", "tok"), None),
        ),
        check_vma=False,
    )
```

time: 174 us -> 161 us (0.925)
  local copies, waits for them, and re-layouts: 8.57 us -> 0 us
  Pallas kernels: 164 us -> 160 us
    unnamed x4 -> x0, local copies, waits for them, and re-layouts: 7.77 us -> none
    pallas_call x1 -> x2, Pallas kernels: 164 us -> 160 us  [the longest x1 157 us: local(): pl.pallas_call(functools.partial(main_kernel, dims), out_shape=out_shape,...]
where the time goes in v1:
time: 161 us; the launch traced here: 160 us
  Pallas kernels  160 us (99%)
    pallas_call x1, Pallas kernels, local(): pl.pallas_call(functools.partial(main_kernel, dims), out_shape=out_shape,...  157 us

profile of v1, /device:TPU:0, one launch (start us, length us, event | category | flops | bytes accessed | tf_op | source)
XLA Modules:
  0.0 160.5 jit_solution(17751616554329452352)
XLA Ops:
  0.6 157.0 %branch_backward.1 = (bf16[4,128,768]{2,1,0:T(8,128)(2,1)}, bf16[4,128,768]{2,1,0:T(8,128)(2,1)}, bf16[4,128,768]{2,1,0:T(8,128)(2,1)}, f32[48,768]{1,0:T(8,128)}) custom-call(s32[16]{0:T(128)} %off_ref.1, bf16[4,128,768]{2,1,0:T(8,128)(2,1)} %q_hbm.1, bf16[4,128,768]{2,1,0:T(8,128)(2,1)} %k_hbm.1, bf16[4,128,768]{2,1,0:T(8,128)(2,1)} %v_hbm.1, ...), custom_call_target="tpu_custom_call" | custom-call | tf_op jit(solution)/shard_map/branch_backward/pallas_call | solution.py:336
  157.7 2.6 %hand_over.1 = (bf16[4,128,768]{2,1,0:T(8,128)(2,1)}, bf16[4,128,768]{2,1,0:T(8,128)(2,1)}, bf16[4,128,768]{2,1,0:T(8,128)(2,1)}, f32[48,768]{1,0:T(8,128)}) custom-call(bf16[4,128,768]{2,1,0:T(8,128)(2,1)} %get-tuple-element.8.refs_0_, bf16[4,128,768]{2,1,0:T(8,128)(2,1)} %get-tuple-element.9.refs_1_, bf16[4,128,768]{2,1,0:T(8,128)(2,1)} %get-tuple-element.10.refs_2_, ...), custom_call_target="tpu_custom_call" | custom-call | tf_op jit(solution)/shard_map/hand_over/pallas_call | solution.py:386

commit v2 on v1

--- a/solution.py
+++ b/solution.py
@@ -44,6 +44,11 @@
     lane = me % heads
     base = me - lane
     order = sorted(range(1, heads), key=lambda s: (-(s // (heads // 2)), -s))
+    across = [s for s in order if s >= heads // 2]
+    within = [s for s in order if s < heads // 2]
+    quarter = lane // (heads // 4)
+    outer = jnp.logical_or(quarter == 0, quarter == 3)
+    inner = jnp.logical_not(outer)
     scale = head_dim ** (-0.5)
     group = heads // 2
     groups = tok // group
@@ -77,8 +82,8 @@
     def columns(d):
         return pl.ds(pl.multiple_of(d * rows, rows), rows)
 
-    def send_out(r, first, count, send_sem, recv_sem):
-        for s in order:
+    def send_to(peers, r, first, count, send_sem, recv_sem):
+        for s in peers:
             d = flip_bits(lane, s)
             pltpu.make_async_remote_copy(
                 src_ref=out_t.at[r, pl.ds(first, count), d],
@@ -88,6 +93,12 @@
                 device_id={"tok": base + d},
                 device_id_type=MESH,
             ).start()
+
+    def send_across(r, first, count, send_sem, recv_sem):
+        send_to(across, r, first, count, send_sem, recv_sem)
+
+    def send_within(r, first, count, send_sem, recv_sem):
+        send_to(within, r, first, count, send_sem, recv_sem)
         pltpu.make_async_copy(
             out_t.at[r, pl.ds(first, count), lane],
             recv.at[r, pl.ds(first, count), :, columns(lane)],
@@ -117,39 +128,75 @@
     for h in range(heads):
         perm[h * PACK : (h + 1) * PACK, :] = jnp.where(at == off_ref[h], 1.0, 0.0).astype(BF16)
     pl.semaphore_wait(barrier, len(greet))
-    send_out(0, 0, 3, qkv_send, qkv_recv)
+
+    @pl.when(outer)
+    def _():
+        send_across(0, 0, 3, qkv_send, qkv_recv)
+
+    send_within(0, 0, 3, qkv_send, qkv_recv)
+
+    @pl.when(inner)
+    def _():
+        send_across(0, 0, 3, qkv_send, qkv_recv)
+
     load_w.wait()
     wt[...] = w[...].T
 
     def prepare(r, carry):
         project(r)
-        send_out(r, 3, 1, g_send, g_recv)
+
+        @pl.when(jnp.logical_and(r == 0, outer))
+        def _():
+            send_across(r, 3, 1, g_send, g_recv)
+
+        send_within(r, 3, 1, g_send, g_recv)
+
+        @pl.when(inner)
+        def _():
+            send_across(r, 3, 1, g_send, g_recv)
 
         @pl.when(r + 1 < rounds)
         def _():
             turn(r + 1)
-            send_out(r + 1, 0, 3, qkv_send, qkv_recv)
+            send_within(r + 1, 0, 3, qkv_send, qkv_recv)
+
+            @pl.when(inner)
+            def _():
+                send_across(r + 1, 0, 3, qkv_send, qkv_recv)
 
         return carry
 
     lax.fori_loop(0, rounds, prepare, 0)
 
     def send_back(r, a, send_sem, recv_sem):
-        for s in order:
-            d = flip_bits(lane, s)
-            pltpu.make_async_remote_copy(
-                src_ref=res.at[r, a, :, columns(d)],
-                dst_ref=ret.at[r, a, lane],
-                send_sem=send_sem,
-                recv_sem=recv_sem,
-                device_id={"tok": base + d},
-                device_id_type=MESH,
-            ).start()
+        def send_to_all(peers):
+            for s in peers:
+                d = flip_bits(lane, s)
+                pltpu.make_async_remote_copy(
+                    src_ref=res.at[r, a, :, columns(d)],
+                    dst_ref=ret.at[r, a, lane],
+                    send_sem=send_sem,
+                    recv_sem=recv_sem,
+                    device_id={"tok": base + d},
+                    device_id_type=MESH,
+                ).start()
+
+        @pl.when(outer)
+        def _():
+            send_to_all(across)
+
+        send_to_all(within)
         pltpu.make_async_copy(res.at[r, a, :, columns(lane)], ret.at[r, a, lane], recv_sem).start()
 
-    def send_grads(r):
-        for a in range(3):
-            send_back(r, a, res_send.at[r, a], ret_recv.at[r, a])
+        @pl.when(inner)
+        def _():
+            send_to_all(across)
+
+    def send_attn(r):
+        send_back(r, 3, attn_send.at[r], attn_recv.at[r])
+
+    def send_grad(r, a):
+        send_back(r, a, res_send.at[r, a], ret_recv.at[r, a])
 
     block = seg // 2
     k_pad = jnp.zeros((LANES - 2 * head_dim, seg), BF16)
@@ -159,14 +206,29 @@
     def attend(r, carry):
         got = recv.at[r, pl.ds(0, 3)]
         pltpu.make_async_copy(got, got, qkv_recv.at[r]).wait()
+        pltpu.make_async_copy(recv.at[r, 3], recv.at[r, 3], g_recv.at[r]).wait()
+
+        @pl.when(jnp.logical_and(outer, r + 1 < rounds))
+        def _():
+            send_across(r + 1, 0, 3, qkv_send, qkv_recv)
+            send_across(r + 1, 3, 1, g_send, g_recv)
+
+        @pl.when(r == rounds - 2)
+        def _():
+            def one(i, inner_carry):
+                send_attn(i)
+                return inner_carry
+
+            lax.fori_loop(0, rounds - 2, one, 0)
+            send_grad(0, 0)
+            send_grad(0, 1)
+
         kt = recv[r, 1]
         vt = recv[r, 2]
         kk[...] = jnp.concatenate([kt, kt, k_pad], 0).T
         vv[...] = jnp.concatenate([vt, ones, v_pad], 0).T
         vt1[...] = jnp.concatenate([vt, ones], 0)
         acc[...] = jnp.zeros_like(acc)
-        pltpu.make_async_copy(recv.at[r, 3], recv.at[r, 3], g_recv.at[r]).wait()
-
         def q_block(b, inner):
             cols = pl.ds(pl.multiple_of(b * block, block), block)
             qt = recv[r, 0, :, cols].astype(F32)
@@ -204,19 +266,25 @@
             return inner
 
         lax.fori_loop(0, seg // block, q_block, 0)
-        send_back(r, 3, attn_send.at[r], attn_recv.at[r])
+
+        @pl.when(r >= rounds - 2)
+        def _():
+            send_attn(r)
+
         t = acc[...].astype(BF16).T
         res[r, 2] = t[:head_dim]
         res[r, 1] = t[head_dim : 2 * head_dim]
 
-        @pl.when(r == 1)
-        def _():
-            send_grads(0)
+        @pl.when(r == rounds - 2)
+        def _():
+            send_grad(0, 2)
 
         return carry
 
     lax.fori_loop(0, rounds, attend, 0)
-    send_grads(1)
+    later = [(r, a) for r in range(rounds) for a in range(3)][3:]
+    for piece in later[:3]:
+        send_grad(*piece)
 
     term[...] = jnp.zeros_like(term)
 
@@ -258,10 +326,13 @@
             laid[r, a] = ret[r, a].reshape(width, rows).T
             pltpu.make_async_copy(laid.at[r, a], ref.at[r], out_sem.at[r, a]).start()
 
+    beside = later[3:8]
     for s in range(1, group):
         near(s).start()
-    for r in range(2, rounds - 1):
-        send_grads(r)
+        for piece in beside[(s - 1) * len(beside) // (group - 1) : s * len(beside) // (group - 1)]:
+            send_grad(*piece)
+    for piece in later[8:9]:
+        send_grad(*piece)
     lay_out(0)
     for s in range(1, group):
         near(s).wait()
@@ -273,7 +344,8 @@
         cross_out[j] = total.astype(BF16)
     for s in range(1, groups):
         far(s).start()
-    send_grads(rounds - 1)
+    for piece in later[9:]:
+        send_grad(*piece)
     for r in range(1, rounds - 1):
         lay_out(r)
     for s in range(1, groups):

time: 161 us -> 156 us (0.969)
  Pallas kernels: 160 us -> 155 us
    pallas_call x1, Pallas kernels: 157 us -> 152 us  [local(): pl.pallas_call(functools.partial(main_kernel, dims), out_shape=out_shape,...]
where the time goes in v2:
time: 156 us; the launch traced here: 155 us
  Pallas kernels  155 us (99%)
    pallas_call x1, Pallas kernels, local(): pl.pallas_call(functools.partial(main_kernel, dims), out_shape=out_shape,...  152 us

profile of v2, /device:TPU:0, one launch (start us, length us, event | category | flops | bytes accessed | tf_op | source)
XLA Modules:
  0.0 155.4 jit_solution(3961788011008693288)
XLA Ops:
  0.6 151.9 %branch_backward.1 = (bf16[4,128,768]{2,1,0:T(8,128)(2,1)}, bf16[4,128,768]{2,1,0:T(8,128)(2,1)}, bf16[4,128,768]{2,1,0:T(8,128)(2,1)}, f32[48,768]{1,0:T(8,128)}) custom-call(s32[16]{0:T(128)} %off_ref.1, bf16[4,128,768]{2,1,0:T(8,128)(2,1)} %q_hbm.1, bf16[4,128,768]{2,1,0:T(8,128)(2,1)} %k_hbm.1, bf16[4,128,768]{2,1,0:T(8,128)(2,1)} %v_hbm.1, ...), custom_call_target="tpu_custom_call" | custom-call | tf_op jit(solution)/shard_map/branch_backward/pallas_call | solution.py:408
  152.6 2.6 %hand_over.1 = (bf16[4,128,768]{2,1,0:T(8,128)(2,1)}, bf16[4,128,768]{2,1,0:T(8,128)(2,1)}, bf16[4,128,768]{2,1,0:T(8,128)(2,1)}, f32[48,768]{1,0:T(8,128)}) custom-call(bf16[4,128,768]{2,1,0:T(8,128)(2,1)} %get-tuple-element.8.refs_0_, bf16[4,128,768]{2,1,0:T(8,128)(2,1)} %get-tuple-element.9.refs_1_, bf16[4,128,768]{2,1,0:T(8,128)(2,1)} %get-tuple-element.10.refs_2_, ...), custom_call_target="tpu_custom_call" | custom-call | tf_op jit(solution)/shard_map/hand_over/pallas_call | solution.py:458

commit v3 on v2

--- a/solution.py
+++ b/solution.py
@@ -33,10 +33,10 @@
     dims,
     off_ref, q_hbm, k_hbm, v_hbm, w_hbm, x_hbm,
     dq_hbm, dk_hbm, dv_hbm, gw_hbm,
-    x, qkv, w, wt, perm, out_t, recv, res, ret, kk, vv, vt1, acc, term, part, half, landed, cross_out, cross_in,
+    x, qkv, w, wt, perm, out_t, recv, res, ret, kk, vv, vt1, acc, term, part, half, pair_in, near_out, landed, cross_out, cross_in, mine,
     laid, gw,
     x_sem, in_sem, w_sem, qkv_send, qkv_recv, g_send, g_recv, res_send, ret_recv, attn_send, attn_recv,
-    red_send, red_recv, cross_send, cross_recv, out_sem, gw_sem,
+    pair_send, pair_recv, red_send, red_recv, cross_send, cross_recv, out_sem, gw_sem,
 ):
     rounds, rows, width, heads, head_dim, tok, phases = dims
     seg = heads * rows
@@ -54,6 +54,9 @@
     groups = tok // group
     lo = me % group
     hi = me // group
+    chip = lo // 2
+    core = lo % 2
+    chips = group // 2
     own = width // tok
     chunks = rows // PACK
 
@@ -297,16 +300,24 @@
         return carry
 
     lax.fori_loop(0, rounds, finish, 0)
-    part[...] = term[...].T.reshape(groups, group, own, width)
+    part[...] = term[...].T.reshape(groups, chips, 2, own, width)
     half[...] = part[...].astype(BF16)
+    pair = pltpu.make_async_remote_copy(
+        src_ref=half.at[:, :, 1 - core],
+        dst_ref=pair_in,
+        send_sem=pair_send,
+        recv_sem=pair_recv,
+        device_id={"tok": me + 1 - 2 * core},
+        device_id_type=MESH,
+    )
 
     def near(s):
         return pltpu.make_async_remote_copy(
-            src_ref=half.at[:, flip_bits(lo, s)],
-            dst_ref=landed.at[lo],
+            src_ref=near_out.at[:, flip_bits(chip, s)],
+            dst_ref=landed.at[chip],
             send_sem=red_send.at[s],
             recv_sem=red_recv.at[s],
-            device_id={"tok": hi * group + flip_bits(lo, s)},
+            device_id={"tok": hi * group + flip_bits(chip, s) * 2 + core},
             device_id_type=MESH,
         )
 
@@ -326,21 +337,29 @@
             laid[r, a] = ret[r, a].reshape(width, rows).T
             pltpu.make_async_copy(laid.at[r, a], ref.at[r], out_sem.at[r, a]).start()
 
-    beside = later[3:8]
-    for s in range(1, group):
+    pair.start()
+    for piece in later[3:6]:
+        send_grad(*piece)
+    pair.wait()
+    for j in range(groups):
+        for u in range(chips):
+            near_out[j, u] = (part[j, u, core] + pair_in[j, u].astype(F32)).astype(BF16)
+        mine[j] = part[j, chip, core] + pair_in[j, chip].astype(F32)
+    beside = later[6:9]
+    for s in range(1, chips):
         near(s).start()
-        for piece in beside[(s - 1) * len(beside) // (group - 1) : s * len(beside) // (group - 1)]:
+        for piece in beside[(s - 1) * len(beside) // (chips - 1) : s * len(beside) // (chips - 1)]:
             send_grad(*piece)
-    for piece in later[8:9]:
+    for piece in later[9:9]:
         send_grad(*piece)
     lay_out(0)
-    for s in range(1, group):
+    for s in range(1, chips):
         near(s).wait()
     for j in range(groups):
-        total = part[j, lo]
-        for s in range(1, group):
-            total = total + landed[flip_bits(lo, s), j].astype(F32)
-        part[j, lo] = total
+        total = mine[j]
+        for s in range(1, chips):
+            total = total + landed[flip_bits(chip, s), j].astype(F32)
+        mine[j] = total
         cross_out[j] = total.astype(BF16)
     for s in range(1, groups):
         far(s).start()
@@ -350,7 +369,7 @@
         lay_out(r)
     for s in range(1, groups):
         far(s).wait()
-    total = part[hi, lo]
+    total = mine[hi]
     for s in range(1, groups):
         total = total + cross_in[flip_bits(hi, s)].astype(F32)
     gw[...] = total
@@ -425,11 +444,14 @@
             pltpu.VMEM((head_dim + PACK, seg), BF16),
             pltpu.VMEM((seg, LANES), F32),
             pltpu.VMEM((width, width), F32),
-            pltpu.VMEM((groups, group, own, width), F32),
-            pltpu.VMEM((groups, group, own, width), BF16),
-            pltpu.VMEM((group, groups, own, width), BF16),
+            pltpu.VMEM((groups, group // 2, 2, own, width), F32),
+            pltpu.VMEM((groups, group // 2, 2, own, width), BF16),
+            pltpu.VMEM((groups, group // 2, own, width), BF16),
+            pltpu.VMEM((groups, group // 2, own, width), BF16),
+            pltpu.VMEM((group // 2, groups, own, width), BF16),
             pltpu.VMEM((groups, own, width), BF16),
             pltpu.VMEM((groups, own, width), BF16),
+            pltpu.VMEM((groups, own, width), F32),
             pltpu.VMEM((rounds, 3, rows, width), BF16),
             pltpu.VMEM((own, width), F32),
             dma((rounds,)),
@@ -443,8 +465,10 @@
             dma((rounds, 3)),
             dma((rounds,)),
             dma((rounds,)),
-            dma((group,)),
-            dma((group,)),
+            dma,
+            dma,
+            dma((group // 2,)),
+            dma((group // 2,)),
             dma((groups,)),
             dma((groups,)),
             dma((rounds, 3)),

time: 156 us -> 154 us (0.987)
  Pallas kernels: 155 us -> 153 us
where the time goes in v3:
time: 154 us
  Pallas kernels  153 us (99%)
    pallas_call x1, Pallas kernels, local(): pl.pallas_call(functools.partial(main_kernel, dims), out_shape=out_shape,...  151 us

profile of v3, /device:TPU:0, one launch (start us, length us, event | category | flops | bytes accessed | tf_op | source)
XLA Modules:
  0.0 154.2 jit_solution(16609571382591336291)
XLA Ops:
  0.6 150.8 %branch_backward.1 = (bf16[4,128,768]{2,1,0:T(8,128)(2,1)}, bf16[4,128,768]{2,1,0:T(8,128)(2,1)}, bf16[4,128,768]{2,1,0:T(8,128)(2,1)}, f32[48,768]{1,0:T(8,128)}) custom-call(s32[16]{0:T(128)} %off_ref.1, bf16[4,128,768]{2,1,0:T(8,128)(2,1)} %q_hbm.1, bf16[4,128,768]{2,1,0:T(8,128)(2,1)} %k_hbm.1, bf16[4,128,768]{2,1,0:T(8,128)(2,1)} %v_hbm.1, ...), custom_call_target="tpu_custom_call" | custom-call | tf_op jit(solution)/shard_map/branch_backward/pallas_call | solution.py:427
  151.4 2.6 %hand_over.1 = (bf16[4,128,768]{2,1,0:T(8,128)(2,1)}, bf16[4,128,768]{2,1,0:T(8,128)(2,1)}, bf16[4,128,768]{2,1,0:T(8,128)(2,1)}, f32[48,768]{1,0:T(8,128)}) custom-call(bf16[4,128,768]{2,1,0:T(8,128)(2,1)} %get-tuple-element.8.refs_0_, bf16[4,128,768]{2,1,0:T(8,128)(2,1)} %get-tuple-element.9.refs_1_, bf16[4,128,768]{2,1,0:T(8,128)(2,1)} %get-tuple-element.10.refs_2_, ...), custom_call_target="tpu_custom_call" | custom-call | tf_op jit(solution)/shard_map/hand_over/pallas_call | solution.py:482

commit v4 on v3

--- a/solution.py
+++ b/solution.py
@@ -125,22 +125,25 @@
             chosen = x[r, :, h * PACK : (h + 1) * PACK, :].reshape(rows, width)
             out_t[r, 3, h] = dot(wt[h * head_dim : (h + 1) * head_dim, :], chosen, 1, 1).astype(BF16)
 
-    turn(0)
     at = lax.broadcasted_iota(jnp.int32, (PACK, PACK * phases), 1)
     at = at - phases * lax.broadcasted_iota(jnp.int32, (PACK, PACK * phases), 0)
     for h in range(heads):
         perm[h * PACK : (h + 1) * PACK, :] = jnp.where(at == off_ref[h], 1.0, 0.0).astype(BF16)
-    pl.semaphore_wait(barrier, len(greet))
-
-    @pl.when(outer)
-    def _():
-        send_across(0, 0, 3, qkv_send, qkv_recv)
-
-    send_within(0, 0, 3, qkv_send, qkv_recv)
-
-    @pl.when(inner)
-    def _():
-        send_across(0, 0, 3, qkv_send, qkv_recv)
+    for a, copy in enumerate(load_qkv(0)):
+        copy.wait()
+        out_t[0, a] = qkv[0, a].T.reshape(heads, head_dim, rows)
+        if a == 0:
+            pl.semaphore_wait(barrier, len(greet))
+
+        @pl.when(outer)
+        def _():
+            send_across(0, a, 1, qkv_send, qkv_recv)
+
+        send_within(0, a, 1, qkv_send, qkv_recv)
+
+        @pl.when(inner)
+        def _():
+            send_across(0, a, 1, qkv_send, qkv_recv)
 
     load_w.wait()
     wt[...] = w[...].T
@@ -225,6 +228,7 @@
             lax.fori_loop(0, rounds - 2, one, 0)
             send_grad(0, 0)
             send_grad(0, 1)
+            send_grad(0, 2)
 
         kt = recv[r, 1]
         vt = recv[r, 2]
@@ -280,13 +284,14 @@
 
         @pl.when(r == rounds - 2)
         def _():
-            send_grad(0, 2)
+            send_grad(1, 0)
+            send_grad(1, 1)
 
         return carry
 
     lax.fori_loop(0, rounds, attend, 0)
-    later = [(r, a) for r in range(rounds) for a in range(3)][3:]
-    for piece in later[:3]:
+    later = [(r, a) for r in range(rounds) for a in range(3)][5:]
+    for piece in later[:2]:
         send_grad(*piece)
 
     term[...] = jnp.zeros_like(term)
@@ -338,19 +343,19 @@
             pltpu.make_async_copy(laid.at[r, a], ref.at[r], out_sem.at[r, a]).start()
 
     pair.start()
-    for piece in later[3:6]:
+    for piece in later[2:4]:
         send_grad(*piece)
     pair.wait()
     for j in range(groups):
         for u in range(chips):
             near_out[j, u] = (part[j, u, core] + pair_in[j, u].astype(F32)).astype(BF16)
         mine[j] = part[j, chip, core] + pair_in[j, chip].astype(F32)
-    beside = later[6:9]
+    beside = later[4:7]
     for s in range(1, chips):
         near(s).start()
         for piece in beside[(s - 1) * len(beside) // (chips - 1) : s * len(beside) // (chips - 1)]:
             send_grad(*piece)
-    for piece in later[9:9]:
+    for piece in later[7:7]:
         send_grad(*piece)
     lay_out(0)
     for s in range(1, chips):
@@ -363,7 +368,7 @@
         cross_out[j] = total.astype(BF16)
     for s in range(1, groups):
         far(s).start()
-    for piece in later[9:]:
+    for piece in later[7:]:
         send_grad(*piece)
     for r in range(1, rounds - 1):
         lay_out(r)
@@ -397,15 +402,20 @@
     count = (len(refs) - 2) // 3
     got, given, kept = refs[:count], refs[count : 2 * count], refs[2 * count : 3 * count]
     in_sem, out_sem = refs[3 * count :]
-    into = [pltpu.make_async_copy(got[i], kept[i], in_sem.at[i]) for i in range(count)]
-    out_of = [pltpu.make_async_copy(kept[i], given[i], out_sem.at[i]) for i in range(count)]
-    for copy in into:
-        copy.start()
-    for i in range(count):
-        into[i].wait()
-        out_of[i].start()
-    for copy in out_of:
-        copy.wait()
+    pieces = [(i, r) for r in range(got[0].shape[0]) for i in range(count - 1)] + [(count - 1, None)]
+
+    def both(n, i, r):
+        a, b, c = (got[i], given[i], kept[i]) if r is None else (got[i].at[r], given[i].at[r], kept[i].at[r])
+        return pltpu.make_async_copy(a, c, in_sem.at[n]), pltpu.make_async_copy(c, b, out_sem.at[n])
+
+    copies = [both(n, i, r) for n, (i, r) in enumerate(pieces)]
+    for into, _ in copies:
+        into.start()
+    for into, out_of in copies:
+        into.wait()
+        out_of.start()
+    for _, out_of in copies:
+        out_of.wait()
 
 
 def local(queries, key_rows, value_rows, projected_output_gradient, out_weight, offsets):
@@ -484,7 +494,7 @@
         out_shape=out_shape,
         in_specs=[hbm] * 4,
         out_specs=(hbm,) * 4,
-        scratch_shapes=[pltpu.VMEM(a.shape, a.dtype) for a in out_shape] + [dma((4,)), dma((4,))],
+        scratch_shapes=[pltpu.VMEM(a.shape, a.dtype) for a in out_shape] + [dma((3 * rounds + 1,)), dma((3 * rounds + 1,))],
         name="hand_over",
     )(*results)
 

time: 154 us -> 152 us (0.987)
  Pallas kernels: 153 us -> 151 us
    pallas_call x1, Pallas kernels: 151 us -> 148 us  [local(): pl.pallas_call(functools.partial(main_kernel, dims), out_shape=out_shape,...]
where the time goes in v4:
time: 152 us; the launch traced here: 151 us
  Pallas kernels  151 us (99%)
    pallas_call x1, Pallas kernels, local(): pl.pallas_call(functools.partial(main_kernel, dims), out_shape=out_shape,...  148 us

profile of v4, /device:TPU:0, one launch (start us, length us, event | category | flops | bytes accessed | tf_op | source)
XLA Modules:
  0.0 151.4 jit_solution(3357302776169838627)
XLA Ops:
  0.6 147.9 %branch_backward.1 = (bf16[4,128,768]{2,1,0:T(8,128)(2,1)}, bf16[4,128,768]{2,1,0:T(8,128)(2,1)}, bf16[4,128,768]{2,1,0:T(8,128)(2,1)}, f32[48,768]{1,0:T(8,128)}) custom-call(s32[16]{0:T(128)} %off_ref.1, bf16[4,128,768]{2,1,0:T(8,128)(2,1)} %q_hbm.1, bf16[4,128,768]{2,1,0:T(8,128)(2,1)} %k_hbm.1, bf16[4,128,768]{2,1,0:T(8,128)(2,1)} %v_hbm.1, ...), custom_call_target="tpu_custom_call" | custom-call | tf_op jit(solution)/shard_map/branch_backward/pallas_call | solution.py:437
  148.5 2.7 %hand_over.1 = (bf16[4,128,768]{2,1,0:T(8,128)(2,1)}, bf16[4,128,768]{2,1,0:T(8,128)(2,1)}, bf16[4,128,768]{2,1,0:T(8,128)(2,1)}, f32[48,768]{1,0:T(8,128)}) custom-call(bf16[4,128,768]{2,1,0:T(8,128)(2,1)} %get-tuple-element.8.refs_0_, bf16[4,128,768]{2,1,0:T(8,128)(2,1)} %get-tuple-element.9.refs_1_, bf16[4,128,768]{2,1,0:T(8,128)(2,1)} %get-tuple-element.10.refs_2_, ...), custom_call_target="tpu_custom_call" | custom-call | tf_op jit(solution)/shard_map/hand_over/pallas_call | solution.py:492

commit v5 on v4

--- a/solution.py
+++ b/solution.py
@@ -372,6 +372,7 @@
         send_grad(*piece)
     for r in range(1, rounds - 1):
         lay_out(r)
+    lay_out(rounds - 1)
     for s in range(1, groups):
         far(s).wait()
     total = mine[hi]
@@ -379,7 +380,6 @@
         total = total + cross_in[flip_bits(hi, s)].astype(F32)
     gw[...] = total
     pltpu.make_async_copy(gw, gw_hbm, gw_sem).start()
-    lay_out(rounds - 1)
 
     for r in range(rounds):
         blocks = pl.ds(0, heads - 1)

time: 152 us -> 151 us (level)
  no operation moved by 1% of the time
where the time goes in v5:
time: 151 us
  Pallas kernels  150 us (99%)
    pallas_call x1, Pallas kernels, local(): pl.pallas_call(functools.partial(main_kernel, dims), out_shape=out_shape,...  148 us

profile of v5, /device:TPU:0, one launch (start us, length us, event | category | flops | bytes accessed | tf_op | source)
XLA Modules:
  0.0 151.0 jit_solution(13204385076027843460)
XLA Ops:
  0.6 147.5 %branch_backward.1 = (bf16[4,128,768]{2,1,0:T(8,128)(2,1)}, bf16[4,128,768]{2,1,0:T(8,128)(2,1)}, bf16[4,128,768]{2,1,0:T(8,128)(2,1)}, f32[48,768]{1,0:T(8,128)}) custom-call(s32[16]{0:T(128)} %off_ref.1, bf16[4,128,768]{2,1,0:T(8,128)(2,1)} %q_hbm.1, bf16[4,128,768]{2,1,0:T(8,128)(2,1)} %k_hbm.1, bf16[4,128,768]{2,1,0:T(8,128)(2,1)} %v_hbm.1, ...), custom_call_target="tpu_custom_call" | custom-call | tf_op jit(solution)/shard_map/branch_backward/pallas_call | solution.py:437
  148.2 2.7 %hand_over.1 = (bf16[4,128,768]{2,1,0:T(8,128)(2,1)}, bf16[4,128,768]{2,1,0:T(8,128)(2,1)}, bf16[4,128,768]{2,1,0:T(8,128)(2,1)}, f32[48,768]{1,0:T(8,128)}) custom-call(bf16[4,128,768]{2,1,0:T(8,128)(2,1)} %get-tuple-element.8.refs_0_, bf16[4,128,768]{2,1,0:T(8,128)(2,1)} %get-tuple-element.9.refs_1_, bf16[4,128,768]{2,1,0:T(8,128)(2,1)} %get-tuple-element.10.refs_2_, ...), custom_call_target="tpu_custom_call" | custom-call | tf_op jit(solution)/shard_map/hand_over/pallas_call | solution.py:492

commit v6 on v5

--- a/solution.py
+++ b/solution.py
@@ -343,14 +343,14 @@
             pltpu.make_async_copy(laid.at[r, a], ref.at[r], out_sem.at[r, a]).start()
 
     pair.start()
-    for piece in later[2:4]:
+    for piece in later[2:5]:
         send_grad(*piece)
     pair.wait()
     for j in range(groups):
         for u in range(chips):
             near_out[j, u] = (part[j, u, core] + pair_in[j, u].astype(F32)).astype(BF16)
         mine[j] = part[j, chip, core] + pair_in[j, chip].astype(F32)
-    beside = later[4:7]
+    beside = later[5:7]
     for s in range(1, chips):
         near(s).start()
         for piece in beside[(s - 1) * len(beside) // (chips - 1) : s * len(beside) // (chips - 1)]:

time: 151 us -> 151 us (level)
  no operation moved by 1% of the time
where the time goes in v6:
time: 151 us
  Pallas kernels  150 us (99%)
    pallas_call x1, Pallas kernels, local(): pl.pallas_call(functools.partial(main_kernel, dims), out_shape=out_shape,...  148 us

profile of v6, /device:TPU:0, one launch (start us, length us, event | category | flops | bytes accessed | tf_op | source)
XLA Modules:
  0.0 151.0 jit_solution(13120238123254126464)
XLA Ops:
  0.6 147.5 %branch_backward.1 = (bf16[4,128,768]{2,1,0:T(8,128)(2,1)}, bf16[4,128,768]{2,1,0:T(8,128)(2,1)}, bf16[4,128,768]{2,1,0:T(8,128)(2,1)}, f32[48,768]{1,0:T(8,128)}) custom-call(s32[16]{0:T(128)} %off_ref.1, bf16[4,128,768]{2,1,0:T(8,128)(2,1)} %q_hbm.1, bf16[4,128,768]{2,1,0:T(8,128)(2,1)} %k_hbm.1, bf16[4,128,768]{2,1,0:T(8,128)(2,1)} %v_hbm.1, ...), custom_call_target="tpu_custom_call" | custom-call | tf_op jit(solution)/shard_map/branch_backward/pallas_call | solution.py:437
  148.2 2.7 %hand_over.1 = (bf16[4,128,768]{2,1,0:T(8,128)(2,1)}, bf16[4,128,768]{2,1,0:T(8,128)(2,1)}, bf16[4,128,768]{2,1,0:T(8,128)(2,1)}, f32[48,768]{1,0:T(8,128)}) custom-call(bf16[4,128,768]{2,1,0:T(8,128)(2,1)} %get-tuple-element.8.refs_0_, bf16[4,128,768]{2,1,0:T(8,128)(2,1)} %get-tuple-element.9.refs_1_, bf16[4,128,768]{2,1,0:T(8,128)(2,1)} %get-tuple-element.10.refs_2_, ...), custom_call_target="tpu_custom_call" | custom-call | tf_op jit(solution)/shard_map/hand_over/pallas_call | solution.py:492
